TPU v7x, 32 devices: a whole 2x2x4 slice. The times are simulated.
32 devices in a mesh: groups: 2 (over y), dp: 4 (over z), tensor: 2 (over x), layer: 2 (over core).
Axes of the slice: x: 2, y: 2, z: 4, core: 2. Of those that a mesh axis runs over, the one named last changes fastest.
Arguments:
- train_inputs: bfloat16 [2, 256, 16, 8192], P('layer', ('groups', 'dp'), None, 'tensor'), parts along dimension 1, may hold values from -6 to 6
- train_grads: bfloat16 [2, 256, 16, 8192], P('layer', ('groups', 'dp'), None, 'tensor'), parts along dimension 1, may hold values from -6 to 6
- bench_inputs: bfloat16 [2, 128, 16, 8192], P('layer', ('groups', 'dp'), None, 'tensor'), parts along dimension 1, may hold values from -6 to 6
- bench_grads: bfloat16 [2, 128, 16, 8192], P('layer', ('groups', 'dp'), None, 'tensor'), parts along dimension 1, may hold values from -6 to 6
- answer_mask: int32 [128, 16], P(('groups', 'dp')), parts along dimension 0, may hold values 0 or 1
- factors: bfloat16 [2, 8192, 128], P('layer', 'tensor'), may hold values from -0.0625 to 0.0625
- precond: bfloat16 [2, 4096, 4096], P('layer', None, ('dp', 'tensor')), may hold values from -0.09375 to 0.09375
Outputs:
- scores: float32 [256, 64], P(('groups', 'dp', 'tensor', 'layer')), parts along dimension 0
There are 2 independent parts, one for each index of `groups`. A program takes and returns all parts, laid end to end along the dimension named above; an argument that names none is the same for every part. Nothing has to cross between parts.
All inputs are finite; a program needn't handle non-finite values. No bound on the sum of `answer_mask` on one device may be relied on, other than what follows from the above.
Results may differ from a plain program's by a relative error of at most 0.005.
Values may be sent and summed in bfloat16 or wider, within the bound.
A program may use at most 64 MiB of HBM per device.

v0:
```python
import math
import jax
import jax.numpy as jnp
from jax import lax
from jax.sharding import PartitionSpec as P


def project(inputs_here, grads_here, factor):
    examples, length, shard_width = inputs_here.shape
    factor_width = factor.shape[1] // 2
    in_proj = jnp.dot(
        inputs_here.reshape(examples * length, shard_width),
        factor[:, :factor_width],
        preferred_element_type=jnp.float32,
    )
    out_proj = jnp.dot(
        grads_here.reshape(examples * length, shard_width),
        factor[:, factor_width:],
        preferred_element_type=jnp.float32,
    )
    return jnp.concatenate([in_proj, out_proj], axis=1)


def outer_features(token_rows, examples, length, factor_width):
    grouped = token_rows.reshape(examples, length, 2 * factor_width)
    outer = jnp.einsum(
        "esa,esb->eab",
        grouped[..., factor_width:],
        grouped[..., :factor_width],
        precision=lax.Precision.HIGHEST,
    ) / math.sqrt(length)
    return outer.reshape(examples, factor_width * factor_width).astype(jnp.bfloat16)


def local(train_inputs, train_grads, bench_inputs, bench_grads, answer_mask, factors, precond):
    factor = factors[0]
    factor_width = factor.shape[1] // 2
    length = train_inputs.shape[2]
    masked = bench_grads[0] * answer_mask.astype(jnp.bfloat16)[:, :, None]
    train_rows = project(train_inputs[0], train_grads[0], factor)
    bench_rows = project(bench_inputs[0], masked, factor)
    tensor_count = lax.axis_size("tensor")
    train_each = train_inputs.shape[1] // tensor_count
    bench_each = bench_inputs.shape[1] // tensor_count
    row_width = train_rows.shape[1]
    blocks = jnp.concatenate(
        [
            train_rows.reshape(tensor_count, train_each * length, row_width),
            bench_rows.reshape(tensor_count, bench_each * length, row_width),
        ],
        axis=1,
    ).reshape(-1, row_width)
    share_rows = blocks.shape[0] // tensor_count
    summed = lax.psum(blocks, "tensor")
    own_rows = lax.dynamic_slice_in_dim(
        summed, lax.axis_index("tensor") * share_rows, share_rows, 0
    )
    train_feats = outer_features(own_rows[: train_each * length], train_each, length, factor_width)
    bench_feats = outer_features(own_rows[train_each * length :], bench_each, length, factor_width)
    columns = precond[0]
    pre_cols = jnp.dot(
        lax.all_gather(bench_feats, ("dp", "tensor"), axis=0, tiled=True),
        columns,
        preferred_element_type=jnp.float32,
    ).astype(jnp.bfloat16)
    layer_total = lax.axis_size("layer") * train_inputs.shape[0]
    score_scale = 1.0 / math.sqrt(factor_width * factor_width * layer_total)
    whole_pre = lax.all_gather(pre_cols, ("dp", "tensor"), axis=1, tiled=True)
    partial_value = jnp.einsum(
        "ek,jk->ej", train_feats, whole_pre, preferred_element_type=jnp.float32
    )
    scores = lax.psum_scatter(partial_value, "layer", scatter_dimension=0, tiled=True)
    return scores * score_scale


def solution(mesh):
    placed = (
        P("layer", ("groups", "dp"), None, "tensor"),
        P("layer", ("groups", "dp"), None, "tensor"),
        P("layer", ("groups", "dp"), None, "tensor"),
        P("layer", ("groups", "dp"), None, "tensor"),
        P(("groups", "dp"), None),
        P("layer", "tensor", None),
        P("layer", None, ("dp", "tensor")),
    )
    return jax.shard_map(
        local,
        mesh=mesh,
        in_specs=placed,
        out_specs=P(("groups", "dp", "tensor", "layer"), None),
        check_vma=False,
    )
```

profile of v0, /device:TPU:0, one launch (start us, length us, event | category | flops | bytes accessed | tf_op | source)
XLA Modules:
  0.0 126.8 jit_solution(3071101061029327510)
XLA Ops:
  6.5 0.0 copy-start
  6.5 0.0 all-reduce.3.cloned.1.call-start
  6.5 0.9 convert_element_type.18
  7.4 0.1 mul.20
  7.5 1.8 %bitcast_multiply_fusion = bf16[256,4096]{1,0:T(8,128)(2,1)S(1)} fusion(bf16[1,16,16,4096]{3,2,1,0:T(8,128)(2,1)} %param.10, bf16[256]{0:T(256)(128)(2,1)S(1)} %mul.20), kind=kLoop, calls=%fused_computation.2 | loop fusion | flops 1048576 | bytes 4194816 | tf_op jit(solution)/shard_map/mul | solution.py:39
  9.3 0.0 copy-done.1
  9.3 1.3 %fusion.7 = f32[256,64]{0,1:T(8,128)S(1)} fusion(bf16[256,4096]{1,0:T(8,128)(2,1)S(1)} %bitcast_multiply_fusion, bf16[4096,128]{1,0:T(8,128)(2,1)S(1)} %bitcast.27), kind=kOutput, calls=%fused_computation.8 | convolution fusion | flops 134217728 | bytes 3211264 | tf_op jit(solution)/shard_map/dot_general | solution.py:16
  10.7 0.8 fusion.11
  11.5 0.1 reshape.25
  11.6 0.0 copy-start.2
  11.6 3.7 %fusion.13 = f32[512,64]{0,1:T(8,128)S(1)} fusion(bf16[512,4096]{1,0:T(8,128)(2,1)} %bitcast.31, bf16[4096,128]{1,0:T(8,128)(2,1)S(1)} %bitcast.29), kind=kOutput, calls=%fused_computation.14 | convolution fusion | flops 268435456 | bytes 5373952 | tf_op jit(solution)/shard_map/dot_general | solution.py:11
  15.3 0.0 copy-done.2
  15.3 0.0 copy-start.3
  15.3 1.7 %fusion.9 = f32[512,64]{0,1:T(8,128)S(1)} fusion(bf16[512,4096]{1,0:T(8,128)(2,1)S(1)} %bitcast.32, bf16[4096,128]{1,0:T(8,128)(2,1)S(1)} %bitcast.30), kind=kOutput, calls=%fused_computation.10 | convolution fusion | flops 268435456 | bytes 5373952 | tf_op jit(solution)/shard_map/dot_general | solution.py:16
  17.1 0.2 reshape.24
  17.3 0.2 pad_maximum_fusion
  17.4 0.9 copy.10
  18.4 0.0 all-reduce.3.cloned.1.call-update
  18.4 0.6 dynamic-slice
  19.7 27.3 %all-reduce.3.cloned.1.call-done = f32[768,128]{1,0:T(8,128)} async-done(((f32[768,128]{1,0:T(8,128)}), f32[768,128]{1,0:T(8,128)}) %all-reduce.3.cloned.1.call-update) | async-done | bytes 393232 | tf_op jit(solution)/shard_map/psum | solution.py:54
  47.0 0.8 constant_dynamic-slice_fusion.1
  47.8 0.7 fusion.3
  48.5 0.2 convert_element_type.22
  48.7 31.4 %all_gather.6 = bf16[64,4096]{1,0:T(8,128)(2,1)S(1)} all-gather(bf16[8,4096]{1,0:T(8,128)(2,1)S(1)} %convert_element_type.22), channel_id=1, replica_groups=mesh['groups'=2,'dp'=4,'tensor'=2,'layer'=2] {'dp','tensor'}, dimensions={0}, use_global_device_ids=true | all-gather | bytes 589824 | tf_op jit(solution)/shard_map/all_gather | solution.py:62
  80.1 3.0 %fusion.4 = bf16[64,512]{1,0:T(8,128)(2,1)S(1)} fusion(bf16[64,4096]{1,0:T(8,128)(2,1)S(1)} %all_gather.6, bf16[1,4096,512]{2,1,0:T(8,128)(2,1)} %param.13), kind=kOutput, calls=%fused_computation.7 | convolution fusion | flops 268468224 | bytes 4784128 | tf_op jit(solution)/shard_map/dot_general | solution.py:61
  83.2 31.2 %all_gather.7 = bf16[64,4096]{1,0:T(8,128)(2,1)S(1)} all-gather(bf16[64,512]{1,0:T(8,128)(2,1)S(1)} %fusion.4), channel_id=1, replica_groups=mesh['groups'=2,'dp'=4,'tensor'=2,'layer'=2] {'dp','tensor'}, dimensions={1}, use_global_device_ids=true | all-gather | bytes 589824 | tf_op jit(solution)/shard_map/all_gather | solution.py:68
  114.4 0.9 constant_dynamic-slice_fusion
  115.3 1.1 fusion.2
  116.4 0.3 convert_element_type.20
  116.7 0.2 fusion.19
  116.9 2.5 %all-reduce = f32[16,64]{1,0:T(8,128)S(1)} all-reduce(f32[16,64]{1,0:T(8,128)S(1)} %fusion.19), channel_id=2, replica_groups=mesh['groups'=2,'dp'=4,'tensor'=2,'layer'=2] {'layer'}, use_global_device_ids=true, to_apply=%region_1.0.clone | all-reduce | flops 1024 | bytes 8192
  119.4 0.6 dynamic-slice_multiply_fusion
  (5 shorter events, 0.0 us)
Async XLA Ops:
  6.5 4.2 %copy-start = (bf16[1,16,16,4096]{3,2,1,0:T(8,128)(2,1)S(1)}, bf16[1,16,16,4096]{3,2,1,0:T(8,128)(2,1)}, u32[]{:S(2)}) copy-start(bf16[1,16,16,4096]{3,2,1,0:T(8,128)(2,1)} %param.9) | copy-start | bytes 6291460
  6.5 2.8 %copy-start.1 = (bf16[1,4096,128]{2,1,0:T(8,128)(2,1)S(1)}, bf16[1,4096,128]{2,1,0:T(8,128)(2,1)}, u32[]{:S(2)}) copy-start(bf16[1,4096,128]{2,1,0:T(8,128)(2,1)} %param.12) | copy-start | bytes 3145732
  6.5 40.5 %all-reduce.3.cloned.1.call-start = ((), (), s32[]{:S(2)}) async-start(), calls=%async_computation | async-start | bytes 786432 | tf_op jit(solution)/shard_map/psum | solution.py:54
  11.6 3.7 %copy-start.2 = (bf16[1,32,16,4096]{3,2,1,0:T(8,128)(2,1)S(1)}, bf16[1,32,16,4096]{3,2,1,0:T(8,128)(2,1)}, u32[]{:S(2)}) copy-start(bf16[1,32,16,4096]{3,2,1,0:T(8,128)(2,1)} %param.8) | copy-start | bytes 12582916
  15.3 3.1 %copy-start.3 = (u32[32]{0:T(128)S(1)}, u32[32]{0:T(128)}, u32[]{:S(2)}) copy-start(u32[32]{0:T(128)} %constant.25) | copy-start | bytes 388
Sparse Core Ops, SparseCore 0:
  18.5 28.4 all-reduce.2
where the time goes:
time: 127 us
  blocking collectives  65.1 us (51%)
  waiting for transfers between devices  27.3 us (21%)
  between operations  14.2 us (11%)
  matrix products  12.6 us (10%)
  local copies, waits for them, and re-layouts  4.08 us (3%)
  other arithmetic  3.48 us (3%)
    all_gather x1, blocking collectives, local(): lax.all_gather(bench_feats, ('dp', 'tensor'), axis=0, tiled=True)  31.4 us
    all_gather x1, blocking collectives, local(): whole_pre = lax.all_gather(pre_cols, ('dp', 'tensor'), axis=1, tiled=True)  31.2 us
    psum x1, waiting for transfers between devices, local(): summed = lax.psum(blocks, 'tensor')  27.3 us
    dot_general x2, matrix products, project(): jnp.dot(inputs_here.reshape(examples * length, shard_width), factor[:, :f...  4.5 us
    dot_general x2, matrix products, project(): jnp.dot(grads_here.reshape(examples * length, shard_width), factor[:, fac...  3.09 us
    dot_general x1, matrix products, local(): jnp.dot(lax.all_gather(bench_feats, ('dp', 'tensor'), axis=0, tiled=True)...  3.02 us
  transfers between devices with their start and end apart: 1, of which 1 were waited for; matrix products, arithmetic and copies ran while one was open for 0% of the time, Pallas kernels for 0%

commit v1 on v0

--- a/solution.py
+++ b/solution.py
@@ -51,7 +51,8 @@
         axis=1,
     ).reshape(-1, row_width)
     share_rows = blocks.shape[0] // tensor_count
-    summed = lax.psum(blocks, "tensor")
+    parts = lax.all_gather(blocks, "tensor")
+    summed = jnp.sum(parts, axis=0)
     own_rows = lax.dynamic_slice_in_dim(
         summed, lax.axis_index("tensor") * share_rows, share_rows, 0
     )

time: 127 us -> 97.2 us (0.77)
  waiting for transfers between devices: 27.3 us -> 0 us
  between operations: 14.2 us -> 0.81 us
  blocking collectives: 65.1 us -> 78.4 us
  local copies, waits for them, and re-layouts: 4.08 us -> 1.6 us
    psum x1 -> x0, waiting for transfers between devices: 27.3 us -> none  [local(): summed = lax.psum(blocks, 'tensor')]
    all_gather x0 -> x1, blocking collectives: none -> 12.7 us  [local(): parts = lax.all_gather(blocks, 'tensor')]
  transfers between devices with their start and end apart: 1 -> 0, of which waited for: 1 -> 0; matrix products, arithmetic and copies ran while one was open for 0% -> 0% of each run, Pallas kernels for 0% -> 0%
where the time goes in v1:
time: 97.2 us; the launch traced here: 96.9 us
  blocking collectives  78.4 us (81%)
  matrix products  12.6 us (13%)
  other arithmetic  3.54 us (4%)
  local copies, waits for them, and re-layouts  1.6 us (2%)
    all_gather x1, blocking collectives, local(): lax.all_gather(bench_feats, ('dp', 'tensor'), axis=0, tiled=True)  31.9 us
    all_gather x1, blocking collectives, local(): whole_pre = lax.all_gather(pre_cols, ('dp', 'tensor'), axis=1, tiled=True)  31.2 us
    all_gather x1, blocking collectives, local(): parts = lax.all_gather(blocks, 'tensor')  12.7 us
    dot_general x2, matrix products, project(): jnp.dot(inputs_here.reshape(examples * length, shard_width), factor[:, :f...  4.5 us
    dot_general x2, matrix products, project(): jnp.dot(grads_here.reshape(examples * length, shard_width), factor[:, fac...  3.09 us
    dot_general x1, matrix products, local(): jnp.dot(lax.all_gather(bench_feats, ('dp', 'tensor'), axis=0, tiled=True)...  3.02 us
    unnamed x1, blocking collectives  2.48 us

profile of v1, /device:TPU:0, one launch (start us, length us, event | category | flops | bytes accessed | tf_op | source)
XLA Modules:
  0.0 96.9 jit_solution(14194496419898839394)
XLA Ops:
  0.0 0.0 copy-start
  0.0 0.0 copy-start.1
  0.0 0.9 convert_element_type.18
  0.9 0.1 mul.20
  1.0 1.8 %bitcast_multiply_fusion = bf16[256,4096]{1,0:T(8,128)(2,1)S(1)} fusion(bf16[1,16,16,4096]{3,2,1,0:T(8,128)(2,1)} %param.10, bf16[256]{0:T(256)(128)(2,1)S(1)} %mul.20), kind=kLoop, calls=%fused_computation.2 | loop fusion | flops 1048576 | bytes 4194816 | tf_op jit(solution)/shard_map/mul | solution.py:39
  2.8 0.0 copy-done.1
  2.8 1.3 %fusion.7 = f32[256,64]{0,1:T(8,128)S(1)} fusion(bf16[256,4096]{1,0:T(8,128)(2,1)S(1)} %bitcast_multiply_fusion, bf16[4096,128]{1,0:T(8,128)(2,1)S(1)} %bitcast.27), kind=kOutput, calls=%fused_computation.8 | convolution fusion | flops 134217728 | bytes 3211264 | tf_op jit(solution)/shard_map/dot_general | solution.py:16
  4.2 0.0 copy-done
  4.2 0.8 fusion.11
  4.9 0.1 reshape.22
  5.0 0.0 copy-start.2
  5.0 3.7 %fusion.13 = f32[512,64]{0,1:T(8,128)S(1)} fusion(bf16[512,4096]{1,0:T(8,128)(2,1)} %bitcast.31, bf16[4096,128]{1,0:T(8,128)(2,1)S(1)} %bitcast.29), kind=kOutput, calls=%fused_computation.14 | convolution fusion | flops 268435456 | bytes 5373952 | tf_op jit(solution)/shard_map/dot_general | solution.py:11
  8.8 0.0 copy-done.2
  8.8 1.7 %fusion.9 = f32[512,64]{0,1:T(8,128)S(1)} fusion(bf16[512,4096]{1,0:T(8,128)(2,1)S(1)} %bitcast.32, bf16[4096,128]{1,0:T(8,128)(2,1)S(1)} %bitcast.30), kind=kOutput, calls=%fused_computation.10 | convolution fusion | flops 268435456 | bytes 5373952 | tf_op jit(solution)/shard_map/dot_general | solution.py:16
  10.5 0.2 reshape.21
  10.7 0.2 pad_maximum_fusion
  10.9 0.2 copy.8
  11.1 12.7 %all_gather.9 = f32[2,768,128]{2,1,0:T(8,128)S(1)} all-gather(f32[1,768,128]{2,1,0:T(8,128)S(1)} %bitcast.33), channel_id=1, replica_groups=mesh['groups'=2,'dp'=4,'tensor'=2,'layer'=2] {'tensor'}, dimensions={0}, use_global_device_ids=true | all-gather | bytes 1179648 | tf_op jit(solution)/shard_map/all_gather | solution.py:54
  23.8 0.1 reduce_sum.9
  23.9 0.0 copy-start.3
  23.9 0.7 fusion.3
  24.6 0.2 convert_element_type.22
  24.8 31.9 %all_gather.10 = bf16[64,4096]{1,0:T(8,128)(2,1)S(1)} all-gather(bf16[8,4096]{1,0:T(8,128)(2,1)S(1)} %convert_element_type.22), channel_id=1, replica_groups=mesh['groups'=2,'dp'=4,'tensor'=2,'layer'=2] {'dp','tensor'}, dimensions={0}, use_global_device_ids=true | all-gather | bytes 589824 | tf_op jit(solution)/shard_map/all_gather | solution.py:63
  56.7 3.0 %fusion.4 = bf16[64,512]{1,0:T(8,128)(2,1)S(1)} fusion(bf16[64,4096]{1,0:T(8,128)(2,1)S(1)} %all_gather.10, bf16[1,4096,512]{2,1,0:T(8,128)(2,1)} %param.13), kind=kOutput, calls=%fused_computation.7 | convolution fusion | flops 268468224 | bytes 4784128 | tf_op jit(solution)/shard_map/dot_general | solution.py:62
  59.8 31.2 %all_gather.11 = bf16[64,4096]{1,0:T(8,128)(2,1)S(1)} all-gather(bf16[64,512]{1,0:T(8,128)(2,1)S(1)} %fusion.4), channel_id=1, replica_groups=mesh['groups'=2,'dp'=4,'tensor'=2,'layer'=2] {'dp','tensor'}, dimensions={1}, use_global_device_ids=true | all-gather | bytes 589824 | tf_op jit(solution)/shard_map/all_gather | solution.py:69
  91.0 1.1 %fusion.2 = bf16[16,64,64]{2,1,0:T(8,128)(2,1)S(1)} fusion(f32[16,16,128]{2,1,0:T(8,128)S(1)} %bitcast.34), kind=kOutput, calls=%fused_computation.4 | convolution fusion | flops 12713984 | bytes 393216 | tf_op jit(solution)/shard_map/esa,esb->eab/dot_general | solution.py:26
  92.1 0.3 convert_element_type.20
  92.4 0.2 fusion.19
  92.6 2.5 %all-reduce = f32[16,64]{1,0:T(8,128)S(1)} all-reduce(f32[16,64]{1,0:T(8,128)S(1)} %fusion.19), channel_id=2, replica_groups=mesh['groups'=2,'dp'=4,'tensor'=2,'layer'=2] {'layer'}, use_global_device_ids=true, to_apply=%region_1.0.clone | all-reduce | flops 1024 | bytes 8192
  95.1 0.0 copy-done.3
  95.1 0.6 dynamic-slice
  96.3 0.6 dynamic-slice_multiply_fusion
  (4 shorter events, 0.1 us)
Async XLA Ops:
  0.0 4.2 %copy-start = (bf16[1,16,16,4096]{3,2,1,0:T(8,128)(2,1)S(1)}, bf16[1,16,16,4096]{3,2,1,0:T(8,128)(2,1)}, u32[]{:S(2)}) copy-start(bf16[1,16,16,4096]{3,2,1,0:T(8,128)(2,1)} %param.9) | copy-start | bytes 6291460
  0.0 2.8 %copy-start.1 = (bf16[1,4096,128]{2,1,0:T(8,128)(2,1)S(1)}, bf16[1,4096,128]{2,1,0:T(8,128)(2,1)}, u32[]{:S(2)}) copy-start(bf16[1,4096,128]{2,1,0:T(8,128)(2,1)} %param.12) | copy-start | bytes 3145732
  5.0 3.7 %copy-start.2 = (bf16[1,32,16,4096]{3,2,1,0:T(8,128)(2,1)S(1)}, bf16[1,32,16,4096]{3,2,1,0:T(8,128)(2,1)}, u32[]{:S(2)}) copy-start(bf16[1,32,16,4096]{3,2,1,0:T(8,128)(2,1)} %param.8) | copy-start | bytes 12582916
  23.9 71.2 %copy-start.3 = (u32[32]{0:T(128)S(1)}, u32[32]{0:T(128)}, u32[]{:S(2)}) copy-start(u32[32]{0:T(128)} %constant.27) | copy-start | bytes 388
